TPU v7x, 256 devices: a whole 4x4x8 slice. The times are simulated.
256 devices in a mesh: tm: 32 (over y_hi, z, core), head: 8 (over y_lo, x).
Axes of the slice: x: 4, y: 4 (y_hi: 2, y_lo: 2; y = y_hi * 2 + y_lo), z: 8, core: 2. Of those that a mesh axis runs over, the one named last changes fastest.
Arguments:
- frames: bfloat16 [16384, 1024], P('tm'), may hold values from -8 to 8
- norm_gain: float32 [1024], replicated, may hold values from 0.5 to 1.5
- w_qkv: bfloat16 [3, 1024, 1024], P(None, 'tm', 'head'), may hold values from -6 to 6
- slopes: float32 [8], P('head'), may hold values from 1.5258789e-05 to 0.05
- w_out: bfloat16 [1024, 1024], P('head', 'tm'), may hold values from -0.5 to 0.5
Outputs:
- attended: bfloat16 [16384, 1024], P(('tm', 'head'))
All inputs are finite; a program needn't handle non-finite values.
Results may differ from a plain program's by a relative error of at most 0.014.
Values may be sent and summed in bfloat16 or wider, within the bound.
No kernel may reach another device: no remote copies, remote signals or barrier semaphores. Data moves between devices by JAX's collectives and lax.ppermute only.
A program may use at most 128 MiB of HBM per device.

v0:
```python
import jax
import jax.numpy as jnp
from jax import lax
from jax.sharding import PartitionSpec as P


def local(frames, norm_gain, w_qkv, slopes, w_out):
    frame_count = frames.shape[0]
    local_heads = slopes.shape[0]
    head_size = w_qkv.shape[2] // local_heads
    tm_count = lax.axis_size("tm")
    clip_len = frame_count * tm_count
    me_tm = lax.axis_index("tm")
    scale = head_size ** (-0.5)
    wide = frames.astype(jnp.float32)
    mean_square = jnp.mean(wide * wide, axis=-1, keepdims=True)
    inverse_root = lax.rsqrt(mean_square + 1e-06)
    normed = (wide * inverse_root * norm_gain).astype(jnp.bfloat16)
    projected = jnp.einsum(
        "rd,cde->cre",
        normed,
        lax.all_gather(w_qkv, "tm", axis=1, tiled=True),
        preferred_element_type=jnp.float32,
    ).astype(jnp.bfloat16)
    query = projected[0].reshape(frame_count, local_heads, head_size)
    keyed = projected[1].reshape(frame_count, local_heads, head_size)
    valued = projected[2].reshape(frame_count, local_heads, head_size)
    row_pos = me_tm * frame_count + jnp.arange(frame_count, dtype=jnp.int32)
    key_piece = lax.all_gather(keyed, "tm", axis=0, tiled=True)
    peak = jnp.full((local_heads, frame_count), -1e30, jnp.float32)
    scores = (
        jnp.einsum("qhd,khd->hqk", query, key_piece, preferred_element_type=jnp.float32) * scale
    )
    key_pos = jnp.arange(key_piece.shape[0], dtype=jnp.int32)
    differ = (key_pos[None, :] - row_pos[:, None]) % clip_len
    distance = jnp.minimum(differ, clip_len - differ).astype(jnp.float32)
    scores = scores - slopes[:, None, None] * distance[None, :, :]
    new_peak = jnp.maximum(peak, jnp.max(scores, axis=-1))
    expo = jnp.exp(scores - new_peak[:, :, None])
    totals = jnp.sum(expo, axis=-1)
    accum = jnp.einsum(
        "hqk,khd->hqd",
        expo.astype(jnp.bfloat16),
        lax.all_gather(valued, "tm", axis=0, tiled=True),
        preferred_element_type=jnp.float32,
    )
    state = (new_peak, totals, accum)
    peak, totals, accum = state
    mixed = (accum / totals[:, :, None]).astype(jnp.bfloat16)
    mixed = jnp.transpose(mixed, (1, 0, 2)).reshape(frame_count, local_heads * head_size)
    out_local = lax.all_gather(w_out, "tm", axis=1, tiled=True)
    return lax.psum_scatter(
        jnp.dot(mixed, out_local, preferred_element_type=jnp.float32).astype(jnp.bfloat16),
        "head",
        scatter_dimension=0,
        tiled=True,
    )


def solution(mesh):
    in_specs = (P("tm", None), P(), P(None, "tm", "head"), P("head"), P("head", "tm"))
    out_specs = P(("tm", "head"), None)
    return jax.shard_map(local, mesh=mesh, in_specs=in_specs, out_specs=out_specs, check_vma=False)
```

profile of v0, /device:TPU:32, one launch (start us, length us, event | category | flops | bytes accessed | tf_op | source)
XLA Modules:
  0.0 288.1 jit_solution(1928262164631459271)
XLA Ops:
  6.5 0.0 all-gather.5.cloned.1.call-start
  6.5 42.6 %all_gather.12 = bf16[3,1024,128]{2,1,0:T(8,128)(2,1)S(1)} all-gather(bf16[3,32,128]{2,1,0:T(8,128)(2,1)} %param.7), channel_id=1, replica_groups=mesh['tm'=32,'head'=8] {'tm'}, dimensions={1}, use_global_device_ids=true | all-gather | bytes 811008 | tf_op jit(solution)/shard_map/all_gather | solution.py:22
  49.2 1.5 fusion.14
  50.7 2.0 fusion.17
  52.7 0.7 fusion.37
  53.4 0.0 all-gather.5.cloned.1.call-update
  53.4 0.0 all-gather.7.cloned.1.call-start
  53.5 0.7 all-gather.7.cloned.1.call-update
  54.2 0.0 reduce-scatter.2.cloned.1.call-start
  54.9 42.0 %all_gather.15 = bf16[128,1024]{0,1:T(8,128)(2,1)S(1)} all-gather(bf16[128,32]{0,1:T(8,128)(2,1)} %param.9), channel_id=1, replica_groups=mesh['tm'=32,'head'=8] {'tm'}, dimensions={1}, use_global_device_ids=true | all-gather | bytes 270336 | tf_op jit(solution)/shard_map/all_gather | solution.py:51
  96.9 41.4 %all-gather.5.cloned.1.call-done = bf16[1,16384,128]{2,1,0:T(8,128)(2,1)} async-done(((bf16[1,512,128]{2,1,0:T(8,128)(2,1)}), bf16[1,16384,128]{2,1,0:T(8,128)(2,1)}) %all-gather.5.cloned.1.call-update) | async-done | bytes 4194320 | tf_op jit(solution)/shard_map/all_gather | solution.py:29
  138.2 29.7 %fusion.38 = (f32[512]{0:T(512)S(1)}, f32[512,16384]{1,0:T(8,128)}) fusion(s32[512]{0:T(512)S(1)} %iota_add_fusion, f32[]{:T(128)} %bitcast.27, bf16[1,16384,128]{2,1,0:T(8,128)(2,1)} %all-gather.5.cloned.1.call-done, bf16[3,512,128]{2,1,0:T(8,128)(2,1)S(1)} %fusion.17), kind=kOutput, calls=%fused_computation.37 | convolution fusion | flops 2306866688 | bytes 37883908 | tf_op jit(solution)/shard_map/qhd,khd->hqk/dot_general | solution.py:32
  168.0 13.8 %fusion.7 = f32[512]{0:T(512)S(1)} fusion(f32[512,16384]{1,0:T(8,128)} %get-tuple-element.8, f32[512]{0:T(512)S(1)} %broadcast_maximum_fusion), kind=kLoop, calls=%fused_computation.12 | loop fusion | flops 16776704 | bytes 33558528 | tf_op jit(solution)/shard_map/reduce_sum | solution.py:40
  181.8 42.5 %all-gather.7.cloned.1.call-done = bf16[1,16384,128]{2,1,0:T(8,128)(2,1)} async-done(((bf16[1,512,128]{2,1,0:T(8,128)(2,1)}), bf16[1,16384,128]{2,1,0:T(8,128)(2,1)}) %all-gather.7.cloned.1.call-update) | async-done | bytes 4194320 | tf_op jit(solution)/shard_map/all_gather | solution.py:44
  224.4 18.0 %convolution_convert_fusion = bf16[512,1024]{1,0:T(8,128)(2,1)} fusion(bf16[128,1024]{0,1:T(8,128)(2,1)S(1)} %all_gather.15, bf16[1,16384,128]{2,1,0:T(8,128)(2,1)} %all-gather.7.cloned.1.call-done, f32[512,16384]{1,0:T(8,128)} %get-tuple-element.8, f32[512]{0:T(512)S(1)} %broadcast_maximum_fusion, f32[512]{0:T(512)S(1)} %fusion.7), kind=kOutput, calls=%fused_computation.23 | convolution fusion | flops 2299133952 | bytes 39063552 | tf_op jit(solution)/shard_map/dot_general | solution.py:53
  242.4 0.0 reduce-scatter.2.cloned.1.call-update
  242.5 39.1 %reduce-scatter.2.cloned.1.call-done = bf16[64,1024]{1,0:T(8,128)(2,1)} async-done(((bf16[512,1024]{1,0:T(8,128)(2,1)}), bf16[64,1024]{1,0:T(8,128)(2,1)}) %reduce-scatter.2.cloned.1.call-update) | async-done | bytes 131088 | tf_op jit(solution)/shard_map/reduce_scatter | solution.py:52
  (3 shorter events, 0.0 us)
Async XLA Ops:
  6.5 131.7 %all-gather.5.cloned.1.call-start = ((), (), s32[]{:S(2)}) async-start(), calls=%async_computation.2 | async-start | bytes 4325376 | tf_op jit(solution)/shard_map/all_gather | solution.py:29
  53.4 171.0 %all-gather.7.cloned.1.call-start = ((), (), s32[]{:S(2)}) async-start(), calls=%async_computation.3 | async-start | bytes 4325376 | tf_op jit(solution)/shard_map/all_gather | solution.py:44
  54.2 227.4 %reduce-scatter.2.cloned.1.call-start = ((), (), s32[]{:S(2)}) async-start(), calls=%async_computation.1 | async-start | bytes 1179648 | tf_op jit(solution)/shard_map/reduce_scatter | solution.py:52
Sparse Core Ops, SparseCore 0:
  53.5 84.6 all-gather.4
  141.0 83.3 all-gather.6
  242.6 38.9 reduce-scatter.1
where the time goes:
time: 288 us
  waiting for transfers between devices  124 us (43%)
  blocking collectives  84.6 us (29%)
  matrix products  49.8 us (17%)
  other arithmetic  15.4 us (5%)
  between operations  13.8 us (5%)
    all_gather x1, blocking collectives, local(): lax.all_gather(w_qkv, 'tm', axis=1, tiled=True)  42.6 us
    all_gather x1, waiting for transfers between devices, local(): lax.all_gather(valued, 'tm', axis=0, tiled=True)  42.5 us
    all_gather x1, blocking collectives, local(): out_local = lax.all_gather(w_out, 'tm', axis=1, tiled=True)  42 us
    all_gather x1, waiting for transfers between devices, local(): key_piece = lax.all_gather(keyed, 'tm', axis=0, tiled=True)  41.4 us
    reduce_scatter x1, waiting for transfers between devices, local(): lax.psum_scatter(jnp.dot(mixed, out_local, preferred_element_type=jnp.flo...  39.1 us
    dot_general x1, matrix products, local(): jnp.einsum('qhd,khd->hqk', query, key_piece, preferred_element_type=jnp.f...  29.7 us
    dot_general x1, matrix products, local(): jnp.dot(mixed, out_local, preferred_element_type=jnp.float32)  18 us
    reduce_sum x1, other arithmetic, local(): totals = jnp.sum(expo, axis=-1)  13.8 us
  transfers between devices with their start and end apart: 3, of which 3 were waited for; matrix products, arithmetic and copies ran while one was open for 15% of the time, Pallas kernels for 0%

commit v1 on v0

--- a/solution.py
+++ b/solution.py
@@ -19,7 +19,9 @@
     projected = jnp.einsum(
         "rd,cde->cre",
         normed,
-        lax.all_gather(w_qkv, "tm", axis=1, tiled=True),
+        jnp.concatenate(
+            lax.all_to_all(jnp.stack([w_qkv] * lax.axis_size("tm")), "tm", 0, 0), axis=1
+        ),
         preferred_element_type=jnp.float32,
     ).astype(jnp.bfloat16)
     query = projected[0].reshape(frame_count, local_heads, head_size)

time: 288 us -> 279 us (0.969)
  blocking collectives: 84.6 us -> 37.7 us
  waiting for transfers between devices: 124 us -> 148 us
  starting transfers between devices: 0.08 us -> 11.5 us
    all_gather x1 -> x0, blocking collectives: 42.6 us -> none  [local(): lax.all_gather(w_qkv, 'tm', axis=1, tiled=True)]
    all_to_all x0 -> x1, waiting for transfers between devices: none -> 23.3 us  [local(): lax.all_to_all(jnp.stack([w_qkv] * lax.axis_size('tm')), 'tm', 0, 0)]
    all_to_all x0 -> x1, starting transfers between devices: none -> 11.4 us  [local(): lax.all_to_all(jnp.stack([w_qkv] * lax.axis_size('tm')), 'tm', 0, 0)]
    all_gather x1, blocking collectives: 42 us -> 37.7 us  [local(): out_local = lax.all_gather(w_out, 'tm', axis=1, tiled=True)]
  transfers between devices with their start and end apart: 3 -> 4, of which waited for: 3 -> 4; matrix products, arithmetic and copies ran while one was open for 15% -> 16% of each run, Pallas kernels for 0% -> 0%
where the time goes in v1:
time: 279 us; the launch traced here: 278 us
  waiting for transfers between devices  148 us (53%)
  matrix products  49.8 us (18%)
  blocking collectives  37.7 us (14%)
  other arithmetic  15.4 us (6%)
  between operations  13.8 us (5%)
  starting transfers between devices  11.5 us (4%)
    all_gather x1, waiting for transfers between devices, local(): lax.all_gather(valued, 'tm', axis=0, tiled=True)  42.5 us
    all_gather x1, waiting for transfers between devices, local(): key_piece = lax.all_gather(keyed, 'tm', axis=0, tiled=True)  42.3 us
    reduce_scatter x1, waiting for transfers between devices, local(): lax.psum_scatter(jnp.dot(mixed, out_local, preferred_element_type=jnp.flo...  39.1 us
    all_gather x1, blocking collectives, local(): out_local = lax.all_gather(w_out, 'tm', axis=1, tiled=True)  37.7 us
    dot_general x1, matrix products, local(): jnp.einsum('qhd,khd->hqk', query, key_piece, preferred_element_type=jnp.f...  29.7 us
    all_to_all x1, waiting for transfers between devices, local(): lax.all_to_all(jnp.stack([w_qkv] * lax.axis_size('tm')), 'tm', 0, 0)  23.3 us
    dot_general x1, matrix products, local(): jnp.dot(mixed, out_local, preferred_element_type=jnp.float32)  18 us
    reduce_sum x1, other arithmetic, local(): totals = jnp.sum(expo, axis=-1)  13.8 us
  transfers between devices with their start and end apart: 4, of which 4 were waited for; matrix products, arithmetic and copies ran while one was open for 16% of the time, Pallas kernels for 0%

profile of v1, /device:TPU:32, one launch (start us, length us, event | category | flops | bytes accessed | tf_op | source)
XLA Modules:
  0.0 278.5 jit_solution(472481001580351591)
XLA Ops:
  6.5 1.7 stack.2
  8.3 11.4 %all-to-all-start = ((bf16[32,3,32,128]{3,2,1,0:T(8,128)(2,1)}), bf16[32,3,32,128]{3,2,1,0:T(8,128)(2,1)S(1)}, u32[]{:S(2)}, u32[]{:S(2)}) async-start(bf16[32,3,32,128]{3,2,1,0:T(8,128)(2,1)} %stack.2), calls=%async_computation | async-start | bytes 1572864 | tf_op jit(solution)/shard_map/all_to_all | solution.py:23
  19.6 0.0 all-gather.5.cloned.1.call-start
  19.7 1.5 fusion.14
  21.2 23.3 %all-to-all-done = bf16[32,3,32,128]{3,2,1,0:T(8,128)(2,1)S(1)} async-done(((bf16[32,3,32,128]{3,2,1,0:T(8,128)(2,1)}), bf16[32,3,32,128]{3,2,1,0:T(8,128)(2,1)S(1)}, u32[]{:S(2)}, u32[]{:S(2)}) %all-to-all-start) | async-done | bytes 786464 | tf_op jit(solution)/shard_map/all_to_all | solution.py:23
  44.5 0.1 copy.6
  44.5 2.0 fusion.17
  46.5 0.7 fusion.37
  47.2 0.0 all-gather.5.cloned.1.call-update
  47.2 0.0 all-gather.7.cloned.1.call-start
  47.3 0.7 all-gather.7.cloned.1.call-update
  48.0 0.0 reduce-scatter.2.cloned.1.call-start
  48.7 37.7 %all_gather.11 = bf16[128,1024]{0,1:T(8,128)(2,1)S(1)} all-gather(bf16[128,32]{0,1:T(8,128)(2,1)} %param.9), channel_id=1, replica_groups=mesh['tm'=32,'head'=8] {'tm'}, dimensions={1}, use_global_device_ids=true | all-gather | bytes 270336 | tf_op jit(solution)/shard_map/all_gather | solution.py:53
  86.4 42.3 %all-gather.5.cloned.1.call-done = bf16[1,16384,128]{2,1,0:T(8,128)(2,1)} async-done(((bf16[1,512,128]{2,1,0:T(8,128)(2,1)}), bf16[1,16384,128]{2,1,0:T(8,128)(2,1)}) %all-gather.5.cloned.1.call-update) | async-done | bytes 4194320 | tf_op jit(solution)/shard_map/all_gather | solution.py:31
  128.7 29.7 %fusion.38 = (f32[512]{0:T(512)S(1)}, f32[512,16384]{1,0:T(8,128)}) fusion(s32[512]{0:T(512)S(1)} %iota_add_fusion, f32[]{:T(128)} %bitcast.29, bf16[1,16384,128]{2,1,0:T(8,128)(2,1)} %all-gather.5.cloned.1.call-done, bf16[3,512,128]{2,1,0:T(8,128)(2,1)S(1)} %fusion.17), kind=kOutput, calls=%fused_computation.37 | convolution fusion | flops 2306866688 | bytes 37883908 | tf_op jit(solution)/shard_map/qhd,khd->hqk/dot_general | solution.py:34
  158.4 13.8 %fusion.7 = f32[512]{0:T(512)S(1)} fusion(f32[512,16384]{1,0:T(8,128)} %get-tuple-element.8, f32[512]{0:T(512)S(1)} %broadcast_maximum_fusion), kind=kLoop, calls=%fused_computation.12 | loop fusion | flops 16776704 | bytes 33558528 | tf_op jit(solution)/shard_map/reduce_sum | solution.py:42
  172.3 42.5 %all-gather.7.cloned.1.call-done = bf16[1,16384,128]{2,1,0:T(8,128)(2,1)} async-done(((bf16[1,512,128]{2,1,0:T(8,128)(2,1)}), bf16[1,16384,128]{2,1,0:T(8,128)(2,1)}) %all-gather.7.cloned.1.call-update) | async-done | bytes 4194320 | tf_op jit(solution)/shard_map/all_gather | solution.py:46
  214.7 18.0 %convolution_convert_fusion = bf16[512,1024]{1,0:T(8,128)(2,1)} fusion(bf16[128,1024]{0,1:T(8,128)(2,1)S(1)} %all_gather.11, bf16[1,16384,128]{2,1,0:T(8,128)(2,1)} %all-gather.7.cloned.1.call-done, f32[512,16384]{1,0:T(8,128)} %get-tuple-element.8, f32[512]{0:T(512)S(1)} %broadcast_maximum_fusion, f32[512]{0:T(512)S(1)} %fusion.7), kind=kOutput, calls=%fused_computation.23 | convolution fusion | flops 2299133952 | bytes 39063552 | tf_op jit(solution)/shard_map/dot_general | solution.py:55
  232.8 0.0 reduce-scatter.2.cloned.1.call-update
  232.8 39.1 %reduce-scatter.2.cloned.1.call-done = bf16[64,1024]{1,0:T(8,128)(2,1)} async-done(((bf16[512,1024]{1,0:T(8,128)(2,1)}), bf16[64,1024]{1,0:T(8,128)(2,1)}) %reduce-scatter.2.cloned.1.call-update) | async-done | bytes 131088 | tf_op jit(solution)/shard_map/reduce_scatter | solution.py:54
  (3 shorter events, 0.0 us)
Async XLA Ops:
  8.3 36.2 %all-to-all-start = ((bf16[32,3,32,128]{3,2,1,0:T(8,128)(2,1)}), bf16[32,3,32,128]{3,2,1,0:T(8,128)(2,1)S(1)}, u32[]{:S(2)}, u32[]{:S(2)}) async-start(bf16[32,3,32,128]{3,2,1,0:T(8,128)(2,1)} %stack.2), calls=%async_computation | async-start | bytes 1572864 | tf_op jit(solution)/shard_map/all_to_all | solution.py:23
  19.6 109.0 %all-gather.5.cloned.1.call-start = ((), (), s32[]{:S(2)}) async-start(), calls=%async_computation.3 | async-start | bytes 4325376 | tf_op jit(solution)/shard_map/all_gather | solution.py:31
  47.2 167.5 %all-gather.7.cloned.1.call-start = ((), (), s32[]{:S(2)}) async-start(), calls=%async_computation.4 | async-start | bytes 4325376 | tf_op jit(solution)/shard_map/all_gather | solution.py:46
  48.0 224.0 %reduce-scatter.2.cloned.1.call-start = ((), (), s32[]{:S(2)}) async-start(), calls=%async_computation.2 | async-start | bytes 1179648 | tf_op jit(solution)/shard_map/reduce_scatter | solution.py:54
Sparse Core Ops, SparseCore 0:
  47.4 81.2 all-gather.4
  131.4 83.2 all-gather.6
  232.9 38.9 reduce-scatter.1
